TPU v7x, 32 devices: a whole 2x2x4 slice. The times are simulated.
32 devices in a mesh: gx: 8 (over y, x, core), gy: 4 (over z).
Axes of the slice: x: 2, y: 2, z: 4, core: 2. Of those that a mesh axis runs over, the one named last changes fastest.
Arguments:
- quotient_table: float32 [32768, 256], P(('gx', 'gy')), may hold values from -6 to 6
- quotient_acc: float32 [32768, 256], P(('gx', 'gy')), may hold values from 1 to 64
- remainder_table: float32 [4096, 256], replicated, may hold values from -6 to 6
- remainder_acc: float32 [4096, 256], P(('gx', 'gy')), may hold values from 1 to 64
- cotangent: bfloat16 [2048, 256], P(('gx', 'gy')), may hold values from -6 to 6
- quotient_ids: int32 [2048, 20], P(('gx', 'gy')), may hold values from 0 to 32767, as said below
- remainder_ids: int32 [2048, 20], P(('gx', 'gy')), may hold values from 0 to 4095
Outputs:
- new_quotient: float32 [32768, 256], P(('gx', 'gy'))
- new_quotient_acc: float32 [32768, 256], P(('gx', 'gy'))
- new_remainder: float32 [4096, 256], replicated
- new_remainder_acc: float32 [4096, 256], P(('gx', 'gy'))
Inputs may be any that keep to these rules, and one draw needn't show every extreme that they name: `quotient_ids`: call the rows k * 1024 to (k + 1) * 1024 - 1 the range of device k along gx+gy. Of the ids of one device's 64 samples, at most 80 fall in any one range; in every draw some range receives exactly 80 from every device.
All inputs are finite; a program needn't handle non-finite values.
Results may differ from a plain program's by a relative error of at most 0.0046.
Values may be sent and summed in bfloat16 or wider, within the bound.
A program may use at most 64 MiB of HBM per device.

v0:
```python
import jax
import jax.numpy as jnp
from jax import lax
from jax.sharding import PartitionSpec as P

LEARNING_RATE = 0.1
EPSILON = 1e-10


def adagrad(param, accum, grad):
    fresh = accum + grad * grad
    return (param - LEARNING_RATE * grad / (jnp.sqrt(fresh) + EPSILON), fresh)


def block_sums(ids, values, count):
    block = count
    if count > 1024 and count % 1024 == 0:
        block = 1024

    def one(first):
        wanted = first + jnp.arange(block, dtype=jnp.int32)
        hit = (wanted[:, None] == ids[None, :]).astype(jnp.bfloat16)
        return jnp.dot(hit, values, preferred_element_type=jnp.float32)

    firsts = jnp.arange(count // block, dtype=jnp.int32) * block
    return lax.map(one, firsts).reshape(count, values.shape[1])


def local(
    quotient_table,
    quotient_acc,
    remainder_table,
    remainder_acc,
    cotangent,
    quotient_ids,
    remainder_ids,
):
    devices = lax.axis_size(("gx", "gy"))
    q_dev, width = quotient_table.shape
    r_rows = remainder_table.shape[0]
    share = remainder_acc.shape[0]
    samples, bag = quotient_ids.shape
    count = samples * bag
    capacity = max(2, (2 * count + devices - 1) // devices)
    table_slots = devices * capacity
    flat_q = quotient_ids.reshape(count)
    flat_r = remainder_ids.reshape(count)
    owner = flat_q // q_dev
    local_row = flat_q - owner * q_dev
    order = jnp.argsort(owner, stable=True)
    sorted_owner = owner[order]
    column = jnp.arange(devices, dtype=jnp.int32)
    tally = jnp.sum((owner[:, None] == column[None, :]).astype(jnp.int32), axis=0)
    begins = jnp.cumsum(tally) - tally
    placed = sorted_owner * capacity + jnp.arange(count, dtype=jnp.int32) - begins[sorted_owner]
    target = jnp.zeros((count,), jnp.int32).at[order].set(placed)
    local_sent = (
        jnp.zeros((table_slots,), jnp.int32).at[target].set(local_row).reshape(devices, capacity)
    )
    cot_rows = jnp.repeat(cotangent, bag, axis=0)
    asked = lax.all_to_all(local_sent, ("gx", "gy"), split_axis=0, concat_axis=0, tiled=True)
    asked_flat = asked.reshape(table_slots)
    found = quotient_table[asked_flat].astype(jnp.bfloat16).reshape(devices, capacity, width)
    replies = lax.all_to_all(found, ("gx", "gy"), split_axis=0, concat_axis=0, tiled=True)
    q_rows = replies.reshape(table_slots, width)[target]
    rem_rows = lax.optimization_barrier(remainder_table[flat_r].astype(jnp.bfloat16))
    cot_wide = cot_rows.astype(jnp.float32)
    q_terms = (cot_wide * rem_rows.astype(jnp.float32)).astype(jnp.bfloat16)
    r_values = (cot_wide * q_rows.astype(jnp.float32)).astype(jnp.bfloat16)
    outgoing = (
        jnp.zeros((table_slots, width), jnp.bfloat16)
        .at[target]
        .set(q_terms)
        .reshape(devices, capacity, width)
    )
    arrived = lax.all_to_all(outgoing, ("gx", "gy"), split_axis=0, concat_axis=0, tiled=True)
    q_values = arrived.reshape(table_slots, width)
    quotient_grad = block_sums(asked_flat, q_values, q_dev)
    new_quotient, new_quotient_acc = adagrad(quotient_table, quotient_acc, quotient_grad)
    first = lax.axis_index(("gx", "gy")) * share
    partial_grad = block_sums(flat_r, r_values, r_rows)
    total = lax.psum(partial_grad, ("gx", "gy"))
    grad_share = lax.dynamic_slice_in_dim(total, first, share, 0)
    param_share = lax.dynamic_slice_in_dim(remainder_table, first, share, 0)
    new_share, new_remainder_acc = adagrad(param_share, remainder_acc, grad_share)
    new_remainder = lax.all_gather(new_share, ("gx", "gy"), axis=0, tiled=True)
    return (new_quotient, new_quotient_acc, new_remainder, new_remainder_acc)


def solution(mesh):
    return jax.shard_map(
        local,
        mesh=mesh,
        in_specs=(
            P(("gx", "gy"), None),
            P(("gx", "gy"), None),
            P(),
            P(("gx", "gy"), None),
            P(("gx", "gy"), None),
            P(("gx", "gy"), None),
            P(("gx", "gy"), None),
        ),
        out_specs=(P(("gx", "gy"), None), P(("gx", "gy"), None), P(), P(("gx", "gy"), None)),
        check_vma=False,
    )
```

profile of v0, /device:TPU:0, one launch (start us, length us, event | category | flops | bytes accessed | tf_op | source)
XLA Modules:
  0.0 350.6 jit_solution(3329541990858526170)
XLA Ops:
  9.9 5.0 %sort.17 = (s32[1280]{0:T(1024)}, s32[1280]{0:T(1024)S(1)}) sort(s32[1280]{0:T(1024)S(1)} %get-tuple-element.98, s32[1280]{0:T(1024)S(1)} %iota.24), dimensions={0}, to_apply=%region_0.1 | sort | flops 14080 | bytes 20480 | tf_op jit(solution)/shard_map/jit(argsort)/sort | solution.py:50
  15.0 7.1 %gather_fusion = s32[1280]{0:T(1024)S(1)} fusion(s32[1280]{0:T(1024)S(1)} %get-tuple-element.98, s32[2048]{0:T(1024)S(1)} %pad_clamp_fusion.3), kind=kCustom, calls=%fused_computation | custom fusion | bytes 15360 | tf_op jit(solution)/shard_map/gather | solution.py:51
  22.1 4.3 %fusion.19 = (s32[1280]{0:T(1024)S(1)}, s32[1280,1]{0,1:T(1,128)S(1)}) fusion(s32[]{:T(128)} %bitcast.28, s32[]{:T(128)} %bitcast.29, s32[]{:T(128)} %bitcast.30, s32[]{:T(128)} %bitcast.31, s32[]{:T(128)} %bitcast.32, s32[]{:T(128)} %bitcast.34, s32[]{:T(128)} %bitcast.33, s32[1280]{0:T(1024)S(1)} %gather_fusion), kind=kLoop, calls=%fused_computation.79 | loop fusion | flops 19200 | bytes 15388 | tf_op jit(solution)/shard_map/gather | solution.py:55
  26.8 15.8 %select_subtract_fusion = s32[1280]{0:T(1024)S(1)} fusion(pred[1280]{0:T(1024)(128)(4,1)S(1)} %get-tuple-element.80, pred[1280]{0:T(1024)(128)(4,1)S(1)} %get-tuple-element.79, pred[1280]{0:T(1024)(128)(4,1)S(1)} %get-tuple-element.78, pred[1280]{0:T(1024)(128)(4,1)S(1)} %get-tuple-element.77, pred[1280]{0:T(1024)(128)(4,1)S(1)} %get-tuple-element.76, ...), kind=kLoop, calls=%fused_computation.73 | loop fusion | flops 35840 | bytes 47460 | tf_op jit(solution)/shard_map/sub | solution.py:55
  42.6 5.2 %scatter_custom_fusion = s32[1280]{0:T(1024)S(1)} fusion(s32[1280]{0:T(1024)S(1)} %compare_select_fusion.4, s32[1280]{0:T(1024)S(1)} %select_subtract_fusion, s32[]{:T(128)} %constant.26.clone.1), kind=kCustom, calls=%fused_computation.81 | custom fusion | bytes 5124 | tf_op jit(solution)/shard_map/scatter | solution.py:56
  47.8 5.3 %scatter_custom_fusion.1 = s32[2560]{0:T(1024)S(1)} fusion(s32[1280]{0:T(1024)S(1)} %compare_select_fusion.3, s32[1280]{0:T(1024)S(1)} %get-tuple-element.97, s32[]{:T(128)} %constant.26.clone.1), kind=kCustom, calls=%fused_computation.77 | custom fusion | bytes 10244 | tf_op jit(solution)/shard_map/scatter | solution.py:58
  53.2 14.3 %all_to_all.19 = s32[32,1,80]{2,1,0:T(1,128)S(1)} all-to-all(s32[32,1,80]{2,1,0:T(1,128)S(1)} %all_to_all.12), channel_id=1, replica_groups=mesh['gx'=8,'gy'=4] {'gx','gy'}, dimensions={0} | all-to-all | bytes 20480 | tf_op jit(solution)/shard_map/all_to_all | solution.py:61
  67.7 6.8 %gather_fusion.2 = bf16[2560,256]{1,0:T(8,128)(2,1)} fusion(f32[1024,256]{1,0:T(8,128)S(1)} %copy-done, s32[3072]{0:T(1024)S(1)} %pad_clamp_fusion), kind=kCustom, calls=%fused_computation.2 | custom fusion | bytes 2631680 | tf_op jit(solution)/shard_map/gather | solution.py:63
  74.5 2.8 all-to-all-start.2
  78.6 2.5 convert_element_type.37
  81.3 26.4 %all-to-all-done.2 = bf16[32,80,256]{2,1,0:T(8,128)(2,1)S(1)} async-done(((bf16[32,80,256]{2,1,0:T(8,128)(2,1)}), bf16[32,80,256]{2,1,0:T(8,128)(2,1)S(1)}, u32[]{:S(2)}, u32[]{:S(2)}) %all-to-all-start.2) | async-done | bytes 1310752 | tf_op jit(solution)/shard_map/all_to_all | solution.py:64
  107.6 4.1 %gather_fusion.3 = bf16[1280,256]{1,0:T(8,128)(2,1)S(1)} fusion(bf16[2560,256]{1,0:T(8,128)(2,1)S(1)} %bitcast.55, s32[2048]{0:T(1024)S(1)} %pad_clamp_fusion.1), kind=kCustom, calls=%fused_computation.3 | custom fusion | bytes 1315840 | tf_op jit(solution)/shard_map/gather | solution.py:65
  113.2 12.5 %while.3 = (s32[]{:T(128)}, f32[4,1024,256]{2,1,0:T(8,128)}, s32[4]{0:T(128)S(1)}, s32[64,20]{1,0:T(8,128)}, bf16[1280,256]{1,0:T(8,128)(2,1)S(1)}, /*index=5*/s32[1280]{0:T(1024)S(1)}, s32[]{:T(128)}) while((s32[]{:T(128)}, f32[4,1024,256]{2,1,0:T(8,128)}, s32[4]{0:T(128)S(1)}, s32[64,20]{1,0:T(8,128)}, ...), condition=%wide.wide.region_7.8_spmd, body=%wide.wide.region_6.7_spmd.sunk | while | flops 672400384 | bytes 1717853 | solution.py:26
  117.5 1.9 fusion.35
  120.7 1.9 fusion.35
  123.8 1.9 fusion.35
  125.8 142.5 %all-reduce.2.cloned.1.call-done = f32[4096,256]{1,0:T(8,128)} async-done(((f32[4096,256]{1,0:T(8,128)}), f32[4096,256]{1,0:T(8,128)}) %all-reduce.2.cloned.1.call-update) | async-done | bytes 4194320 | tf_op jit(solution)/shard_map/psum | solution.py:82
  270.2 5.4 %gather_fusion.1 = bf16[1280,256]{1,0:T(8,128)(2,1)S(1)} fusion(f32[4096,256]{1,0:T(8,128)} %param.11, s32[2048]{0:T(1024)S(1)} %pad_clamp_fusion.2), kind=kCustom, calls=%fused_computation.1 | custom fusion | bytes 1315840 | tf_op jit(solution)/shard_map/gather | solution.py:66
  275.6 9.3 %scatter_custom_fusion.2 = bf16[2560,256]{1,0:T(8,128)(2,1)} fusion(s32[1280]{0:T(1024)S(1)} %compare_select_fusion.3, f32[1280,256]{1,0:T(8,128)S(1)} %copy-done.1, bf16[1280,256]{1,0:T(8,128)(2,1)S(1)} %gather_fusion.1, bf16[]{:T(256)} %constant.39.clone.1), kind=kCustom, calls=%fused_computation.21 | custom fusion | flops 983040 | bytes 3276802 | tf_op jit(solution)/shard_map/scatter | solution.py:73
  284.9 3.9 %all-to-all-start.1 = ((bf16[32,80,256]{2,1,0:T(8,128)(2,1)}), bf16[32,80,256]{2,1,0:T(8,128)(2,1)S(1)}, u32[]{:S(2)}, u32[]{:S(2)}) async-start(bf16[32,80,256]{2,1,0:T(8,128)(2,1)} %bitcast.57), calls=%async_computation.1 | async-start | bytes 2621440 | tf_op jit(solution)/shard_map/all_to_all | solution.py:76
  290.1 39.1 %all-to-all-done.1 = bf16[32,80,256]{2,1,0:T(8,128)(2,1)S(1)} async-done(((bf16[32,80,256]{2,1,0:T(8,128)(2,1)}), bf16[32,80,256]{2,1,0:T(8,128)(2,1)S(1)}, u32[]{:S(2)}, u32[]{:S(2)}) %all-to-all-start.1) | async-done | bytes 1310752 | tf_op jit(solution)/shard_map/all_to_all | solution.py:76
  329.1 4.7 %divide_subtract_fusion = (f32[1024,256]{1,0:T(8,128)}, f32[1024,256]{1,0:T(8,128)}) fusion(f32[1024,256]{1,0:T(8,128)S(1)} %copy-done, f32[1024,256]{1,0:T(8,128)} %param.10, bf16[2560,256]{1,0:T(8,128)(2,1)S(1)} %bitcast.59, s32[2560]{0:T(1024)S(1)} %eq.54), kind=kOutput, calls=%fused_computation.19 | convolution fusion | flops 1346371584 | bytes 5515264 | tf_op jit(solution)/shard_map/while/body/eval_jaxpr/dot_general | solution.py:23
  333.8 5.5 %all-gather.2.cloned.1.call-done = f32[4096,256]{1,0:T(8,128)} async-done(((f32[128,256]{1,0:T(8,128)}), f32[4096,256]{1,0:T(8,128)}) %all-gather.2.cloned.1.call-update) | async-done | bytes 4194320 | tf_op jit(solution)/shard_map/all_gather | solution.py:86
  339.3 4.5 %copy.29 = f32[4096,256]{1,0:T(8,128)} copy(f32[4096,256]{1,0:T(8,128)} %all-gather.2.cloned.1.call-done) | data formatting | bytes 8388608
  (60 shorter events, 16.4 us)
Async XLA Ops:
  15.0 52.7 %copy-start = (f32[1024,256]{1,0:T(8,128)S(1)}, f32[1024,256]{1,0:T(8,128)}, u32[]{:S(2)}) copy-start(f32[1024,256]{1,0:T(8,128)} %param.9) | copy-start | bytes 3145732
  74.5 2.9 copy-start.5
  74.5 33.2 %all-to-all-start.2 = ((bf16[32,80,256]{2,1,0:T(8,128)(2,1)}), bf16[32,80,256]{2,1,0:T(8,128)(2,1)S(1)}, u32[]{:S(2)}, u32[]{:S(2)}) async-start(bf16[32,80,256]{2,1,0:T(8,128)(2,1)} %bitcast.56), calls=%async_computation.2 | async-start | bytes 2621440 | tf_op jit(solution)/shard_map/all_to_all | solution.py:64
  77.3 191.0 %all-reduce.2.cloned.1.call-start = ((), (), s32[]{:S(2)}) async-start(), calls=%async_computation.3 | async-start | bytes 8388608 | tf_op jit(solution)/shard_map/psum | solution.py:82
  78.6 2.5 copy-start.6
  81.1 30.6 %copy-start.2 = (s32[64,20]{1,0:T(8,128)}, s32[64,20]{1,0:T(8,128)S(1)}, u32[]{:S(2)}) copy-start(s32[64,20]{1,0:T(8,128)S(1)} %copy.18) | copy-start | bytes 15364
  125.7 142.6 %copy-start.4 = (f32[128,256]{1,0:T(8,128)S(1)}, f32[128,256]{1,0:T(8,128)}, u32[]{:S(2)}) copy-start(f32[128,256]{1,0:T(8,128)} %param.12) | copy-start | bytes 393220
  125.7 144.3 %copy-start.3 = (s32[64,20]{1,0:T(8,128)S(1)}, s32[64,20]{1,0:T(8,128)}, u32[]{:S(2)}) copy-start(s32[64,20]{1,0:T(8,128)} %get-tuple-element.230) | copy-start | bytes 15364
  125.7 213.6 %all-gather.2.cloned.1.call-start = ((), (), s32[]{:S(2)}) async-start(), calls=%async_computation.4 | async-start | bytes 4325376 | tf_op jit(solution)/shard_map/all_gather | solution.py:86
  270.2 5.4 %copy-start.1 = (f32[1280,256]{1,0:T(8,128)S(1)}, f32[1280,256]{1,0:T(8,128)}, u32[]{:S(2)}) copy-start(f32[1280,256]{1,0:T(8,128)} %convert_element_type.37) | copy-start | bytes 3932164
  284.9 44.2 %all-to-all-start.1 = ((bf16[32,80,256]{2,1,0:T(8,128)(2,1)}), bf16[32,80,256]{2,1,0:T(8,128)(2,1)S(1)}, u32[]{:S(2)}, u32[]{:S(2)}) async-start(bf16[32,80,256]{2,1,0:T(8,128)(2,1)} %bitcast.57), calls=%async_computation.1 | async-start | bytes 2621440 | tf_op jit(solution)/shard_map/all_to_all | solution.py:76
Sparse Core Ops, SparseCore 0:
  125.8 142.3 all-reduce.1
  271.3 68.0 all-gather.1
where the time goes:
time: 352 us; the launch traced here: 351 us
  waiting for transfers between devices  213 us (61%)
  local copies, waits for them, and re-layouts  47.9 us (14%)
  other arithmetic  41.6 us (12%)
  blocking collectives  14.3 us (4%)
  between operations  14.3 us (4%)
  matrix products  12.2 us (3%)
  starting transfers between devices  6.77 us (2%)
    psum x1, waiting for transfers between devices, local(): total = lax.psum(partial_grad, ('gx', 'gy'))  142 us
    all_to_all x1, waiting for transfers between devices, local(): lax.all_to_all(outgoing, ('gx', 'gy'), split_axis=0, concat_axis=0, tiled...  39.1 us
    all_to_all x1, waiting for transfers between devices, local(): lax.all_to_all(found, ('gx', 'gy'), split_axis=0, concat_axis=0, tiled=True)  26.4 us
    sub x1, other arithmetic, local(): sorted_owner * capacity + jnp.arange(count, dtype=jnp.int32)  15.8 us
    all_to_all x1, blocking collectives, local(): lax.all_to_all(local_sent, ('gx', 'gy'), split_axis=0, concat_axis=0, til...  14.3 us
    dot_general x5, matrix products, one(): return jnp.dot(hit, values, preferred_element_type=jnp.float32)  12.2 us
    scatter x1, other arithmetic, local(): outgoing = jnp.zeros((table_slots, width), jnp.bfloat16).at[target].set(q...  9.26 us
    gather x1, local copies, waits for them, and re-layouts, local(): sorted_owner = owner[order]  7.08 us
  transfers between devices with their start and end apart: 4, of which 4 were waited for; matrix products, arithmetic and copies ran while one was open for 7% of the time, Pallas kernels for 0%

commit v1 on v0

--- a/solution.py
+++ b/solution.py
@@ -79,7 +79,7 @@
     new_quotient, new_quotient_acc = adagrad(quotient_table, quotient_acc, quotient_grad)
     first = lax.axis_index(("gx", "gy")) * share
     partial_grad = block_sums(flat_r, r_values, r_rows)
-    total = lax.psum(partial_grad, ("gx", "gy"))
+    total = lax.psum(lax.psum(partial_grad, "gy"), "gx")
     grad_share = lax.dynamic_slice_in_dim(total, first, share, 0)
     param_share = lax.dynamic_slice_in_dim(remainder_table, first, share, 0)
     new_share, new_remainder_acc = adagrad(param_share, remainder_acc, grad_share)

time: 352 us -> 448 us (1.27)
  waiting for transfers between devices: 213 us -> 309 us
    psum x1 -> x2, waiting for transfers between devices: 142 us -> 238 us  [local(): total = lax.psum(lax.psum(partial_grad, 'gy'), 'gx')]
  transfers between devices with their start and end apart: 4 -> 5, of which waited for: 4 -> 5; matrix products, arithmetic and copies ran while one was open for 7% -> 6% of each run, Pallas kernels for 0% -> 0%
where the time goes in v1:
time: 448 us; the launch traced here: 447 us
  waiting for transfers between devices  309 us (69%)
  local copies, waits for them, and re-layouts  48 us (11%)
  other arithmetic  41.6 us (9%)
  blocking collectives  14.3 us (3%)
  between operations  14 us (3%)
  matrix products  12.2 us (3%)
  starting transfers between devices  7.58 us (2%)
    psum x2, waiting for transfers between devices, local(): total = lax.psum(lax.psum(partial_grad, 'gy'), 'gx')  238 us
    all_to_all x1, waiting for transfers between devices, local(): lax.all_to_all(outgoing, ('gx', 'gy'), split_axis=0, concat_axis=0, tiled...  39 us
    all_to_all x1, waiting for transfers between devices, local(): lax.all_to_all(found, ('gx', 'gy'), split_axis=0, concat_axis=0, tiled=True)  26.3 us
    sub x1, other arithmetic, local(): sorted_owner * capacity + jnp.arange(count, dtype=jnp.int32)  15.8 us
    all_to_all x1, blocking collectives, local(): lax.all_to_all(local_sent, ('gx', 'gy'), split_axis=0, concat_axis=0, til...  14.3 us
    dot_general x5, matrix products, one(): return jnp.dot(hit, values, preferred_element_type=jnp.float32)  12.2 us
    scatter x1, other arithmetic, local(): outgoing = jnp.zeros((table_slots, width), jnp.bfloat16).at[target].set(q...  9.26 us
  transfers between devices with their start and end apart: 5, of which 5 were waited for; matrix products, arithmetic and copies ran while one was open for 6% of the time, Pallas kernels for 0%

profile of v1, /device:TPU:0, one launch (start us, length us, event | category | flops | bytes accessed | tf_op | source)
XLA Modules:
  0.0 446.8 jit_solution(3900428368517834728)
XLA Ops:
  9.9 5.0 %sort.17 = (s32[1280]{0:T(1024)}, s32[1280]{0:T(1024)S(1)}) sort(s32[1280]{0:T(1024)S(1)} %get-tuple-element.98, s32[1280]{0:T(1024)S(1)} %iota.24), dimensions={0}, to_apply=%region_0.1 | sort | flops 14080 | bytes 20480 | tf_op jit(solution)/shard_map/jit(argsort)/sort | solution.py:50
  15.0 7.1 %gather_fusion = s32[1280]{0:T(1024)S(1)} fusion(s32[1280]{0:T(1024)S(1)} %get-tuple-element.98, s32[2048]{0:T(1024)S(1)} %pad_clamp_fusion.3), kind=kCustom, calls=%fused_computation | custom fusion | bytes 15360 | tf_op jit(solution)/shard_map/gather | solution.py:51
  22.1 4.3 fusion.19
  26.8 15.8 %select_subtract_fusion = s32[1280]{0:T(1024)S(1)} fusion(pred[1280]{0:T(1024)(128)(4,1)S(1)} %get-tuple-element.80, pred[1280]{0:T(1024)(128)(4,1)S(1)} %get-tuple-element.79, pred[1280]{0:T(1024)(128)(4,1)S(1)} %get-tuple-element.78, pred[1280]{0:T(1024)(128)(4,1)S(1)} %get-tuple-element.77, pred[1280]{0:T(1024)(128)(4,1)S(1)} %get-tuple-element.76, ...), kind=kLoop, calls=%fused_computation.73 | loop fusion | flops 35840 | bytes 47460 | tf_op jit(solution)/shard_map/sub | solution.py:55
  42.6 5.2 %scatter_custom_fusion = s32[1280]{0:T(1024)S(1)} fusion(s32[1280]{0:T(1024)S(1)} %compare_select_fusion.4, s32[1280]{0:T(1024)S(1)} %select_subtract_fusion, s32[]{:T(128)} %constant.26.clone.1), kind=kCustom, calls=%fused_computation.81 | custom fusion | bytes 5124 | tf_op jit(solution)/shard_map/scatter | solution.py:56
  47.8 5.3 %scatter_custom_fusion.1 = s32[2560]{0:T(1024)S(1)} fusion(s32[1280]{0:T(1024)S(1)} %compare_select_fusion.3, s32[1280]{0:T(1024)S(1)} %get-tuple-element.97, s32[]{:T(128)} %constant.26.clone.1), kind=kCustom, calls=%fused_computation.77 | custom fusion | bytes 10244 | tf_op jit(solution)/shard_map/scatter | solution.py:58
  53.2 14.3 %all_to_all.19 = s32[32,1,80]{2,1,0:T(1,128)S(1)} all-to-all(s32[32,1,80]{2,1,0:T(1,128)S(1)} %all_to_all.12), channel_id=1, replica_groups=mesh['gx'=8,'gy'=4] {'gx','gy'}, dimensions={0} | all-to-all | bytes 20480 | tf_op jit(solution)/shard_map/all_to_all | solution.py:61
  67.7 6.8 %gather_fusion.2 = bf16[2560,256]{1,0:T(8,128)(2,1)} fusion(f32[1024,256]{1,0:T(8,128)S(1)} %copy-done, s32[3072]{0:T(1024)S(1)} %pad_clamp_fusion), kind=kCustom, calls=%fused_computation.2 | custom fusion | bytes 2631680 | tf_op jit(solution)/shard_map/gather | solution.py:63
  74.5 2.8 all-to-all-start.2
  78.6 2.6 convert_element_type.37
  81.4 26.3 %all-to-all-done.2 = bf16[32,80,256]{2,1,0:T(8,128)(2,1)S(1)} async-done(((bf16[32,80,256]{2,1,0:T(8,128)(2,1)}), bf16[32,80,256]{2,1,0:T(8,128)(2,1)S(1)}, u32[]{:S(2)}, u32[]{:S(2)}) %all-to-all-start.2) | async-done | bytes 1310752 | tf_op jit(solution)/shard_map/all_to_all | solution.py:64
  107.6 4.1 gather_fusion.3
  113.2 12.5 %while.3 = (s32[]{:T(128)}, f32[4,1024,256]{2,1,0:T(8,128)}, s32[4]{0:T(128)S(1)}, s32[64,20]{1,0:T(8,128)}, bf16[1280,256]{1,0:T(8,128)(2,1)S(1)}, /*index=5*/s32[1280]{0:T(1024)S(1)}, s32[]{:T(128)}) while((s32[]{:T(128)}, f32[4,1024,256]{2,1,0:T(8,128)}, s32[4]{0:T(128)S(1)}, s32[64,20]{1,0:T(8,128)}, ...), condition=%wide.wide.region_7.8_spmd, body=%wide.wide.region_6.7_spmd.sunk | while | flops 672400384 | bytes 1717853 | solution.py:26
  117.5 1.9 fusion.35
  123.8 1.9 fusion.35
  125.8 155.1 %all-reduce.3.cloned.1.call-done = f32[4096,256]{1,0:T(8,128)} async-done(((f32[4096,256]{1,0:T(8,128)}), f32[4096,256]{1,0:T(8,128)}) %all-reduce.3.cloned.1.call-update) | async-done | bytes 4194320 | tf_op jit(solution)/shard_map/psum | solution.py:82
  280.9 83.0 %all-reduce.5.cloned.1.call-done = f32[4096,256]{1,0:T(8,128)} async-done(((f32[4096,256]{1,0:T(8,128)}), f32[4096,256]{1,0:T(8,128)}) %all-reduce.5.cloned.1.call-update) | async-done | bytes 4194320 | tf_op jit(solution)/shard_map/psum | solution.py:82
  365.9 5.4 %gather_fusion.1 = bf16[1280,256]{1,0:T(8,128)(2,1)S(1)} fusion(f32[4096,256]{1,0:T(8,128)} %param.11, s32[2048]{0:T(1024)S(1)} %pad_clamp_fusion.2), kind=kCustom, calls=%fused_computation.1 | custom fusion | bytes 1315840 | tf_op jit(solution)/shard_map/gather | solution.py:66
  371.3 9.3 %scatter_custom_fusion.2 = bf16[2560,256]{1,0:T(8,128)(2,1)} fusion(s32[1280]{0:T(1024)S(1)} %compare_select_fusion.3, f32[1280,256]{1,0:T(8,128)S(1)} %copy-done.1, bf16[1280,256]{1,0:T(8,128)(2,1)S(1)} %gather_fusion.1, bf16[]{:T(256)} %constant.39.clone.1), kind=kCustom, calls=%fused_computation.21 | custom fusion | flops 983040 | bytes 3276802 | tf_op jit(solution)/shard_map/scatter | solution.py:73
  380.6 4.7 %all-to-all-start.1 = ((bf16[32,80,256]{2,1,0:T(8,128)(2,1)}), bf16[32,80,256]{2,1,0:T(8,128)(2,1)S(1)}, u32[]{:S(2)}, u32[]{:S(2)}) async-start(bf16[32,80,256]{2,1,0:T(8,128)(2,1)} %bitcast.57), calls=%async_computation.1 | async-start | bytes 2621440 | tf_op jit(solution)/shard_map/all_to_all | solution.py:76
  386.5 39.0 %all-to-all-done.1 = bf16[32,80,256]{2,1,0:T(8,128)(2,1)S(1)} async-done(((bf16[32,80,256]{2,1,0:T(8,128)(2,1)}), bf16[32,80,256]{2,1,0:T(8,128)(2,1)S(1)}, u32[]{:S(2)}, u32[]{:S(2)}) %all-to-all-start.1) | async-done | bytes 1310752 | tf_op jit(solution)/shard_map/all_to_all | solution.py:76
  425.5 4.7 %divide_subtract_fusion = (f32[1024,256]{1,0:T(8,128)}, f32[1024,256]{1,0:T(8,128)}) fusion(f32[1024,256]{1,0:T(8,128)S(1)} %copy-done, f32[1024,256]{1,0:T(8,128)} %param.10, bf16[2560,256]{1,0:T(8,128)(2,1)S(1)} %bitcast.59, s32[2560]{0:T(1024)S(1)} %eq.54), kind=kOutput, calls=%fused_computation.19 | convolution fusion | flops 1346371584 | bytes 5515264 | tf_op jit(solution)/shard_map/while/body/eval_jaxpr/dot_general | solution.py:23
  430.2 5.6 %all-gather.2.cloned.1.call-done = f32[4096,256]{1,0:T(8,128)} async-done(((f32[128,256]{1,0:T(8,128)}), f32[4096,256]{1,0:T(8,128)}) %all-gather.2.cloned.1.call-update) | async-done | bytes 4194320 | tf_op jit(solution)/shard_map/all_gather | solution.py:86
  435.8 4.5 %copy.30 = f32[4096,256]{1,0:T(8,128)} copy(f32[4096,256]{1,0:T(8,128)} %all-gather.2.cloned.1.call-done) | data formatting | bytes 8388608
  (63 shorter events, 18.3 us)
Async XLA Ops:
  15.0 52.7 %copy-start = (f32[1024,256]{1,0:T(8,128)S(1)}, f32[1024,256]{1,0:T(8,128)}, u32[]{:S(2)}) copy-start(f32[1024,256]{1,0:T(8,128)} %param.9) | copy-start | bytes 3145732
  74.5 2.9 copy-start.5
  74.5 33.2 %all-to-all-start.2 = ((bf16[32,80,256]{2,1,0:T(8,128)(2,1)}), bf16[32,80,256]{2,1,0:T(8,128)(2,1)S(1)}, u32[]{:S(2)}, u32[]{:S(2)}) async-start(bf16[32,80,256]{2,1,0:T(8,128)(2,1)} %bitcast.56), calls=%async_computation.2 | async-start | bytes 2621440 | tf_op jit(solution)/shard_map/all_to_all | solution.py:64
  77.3 203.6 %all-reduce.3.cloned.1.call-start = ((), (), s32[]{:S(2)}) async-start(), calls=%async_computation.3 | async-start | bytes 8388608 | tf_op jit(solution)/shard_map/psum | solution.py:82
  78.6 2.6 copy-start.6
  81.2 30.4 %copy-start.2 = (s32[64,20]{1,0:T(8,128)}, s32[64,20]{1,0:T(8,128)S(1)}, u32[]{:S(2)}) copy-start(s32[64,20]{1,0:T(8,128)S(1)} %copy.18) | copy-start | bytes 15364
  125.7 238.2 %all-reduce.5.cloned.1.call-start = ((), (), s32[]{:S(2)}) async-start(), calls=%async_computation.4 | async-start | bytes 8388608 | tf_op jit(solution)/shard_map/psum | solution.py:82
  280.9 83.1 %copy-start.4 = (f32[128,256]{1,0:T(8,128)S(1)}, f32[128,256]{1,0:T(8,128)}, u32[]{:S(2)}) copy-start(f32[128,256]{1,0:T(8,128)} %param.12) | copy-start | bytes 393220
  280.9 84.8 %copy-start.3 = (s32[64,20]{1,0:T(8,128)S(1)}, s32[64,20]{1,0:T(8,128)}, u32[]{:S(2)}) copy-start(s32[64,20]{1,0:T(8,128)} %get-tuple-element.234) | copy-start | bytes 15364
  280.9 154.9 %all-gather.2.cloned.1.call-start = ((), (), s32[]{:S(2)}) async-start(), calls=%async_computation.5 | async-start | bytes 4325376 | tf_op jit(solution)/shard_map/all_gather | solution.py:86
  365.9 5.4 %copy-start.1 = (f32[1280,256]{1,0:T(8,128)S(1)}, f32[1280,256]{1,0:T(8,128)}, u32[]{:S(2)}) copy-start(f32[1280,256]{1,0:T(8,128)} %convert_element_type.37) | copy-start | bytes 3932164
  380.6 45.0 %all-to-all-start.1 = ((bf16[32,80,256]{2,1,0:T(8,128)(2,1)}), bf16[32,80,256]{2,1,0:T(8,128)(2,1)S(1)}, u32[]{:S(2)}, u32[]{:S(2)}) async-start(bf16[32,80,256]{2,1,0:T(8,128)(2,1)} %bitcast.57), calls=%async_computation.1 | async-start | bytes 2621440 | tf_op jit(solution)/shard_map/all_to_all | solution.py:76
Sparse Core Ops, SparseCore 0:
  125.8 154.9 all-reduce.2
  284.1 79.7 all-reduce.4
  367.0 68.8 all-gather.1
